TPU v7x, 32 devices: a whole 2x2x4 slice. The times are simulated.
32 devices in a mesh: replica: 4 (over y, x), fsdp: 2 (over core), tensor: 4 (over z).
Axes of the slice: x: 2, y: 2, z: 4, core: 2. Of those that a mesh axis runs over, the one named last changes fastest.
Arguments:
- attn_out: bfloat16 [2048, 8192], P(('replica', 'tensor'), 'fsdp'), may hold values from -6 to 6
- out_grad: bfloat16 [2048, 8192], P(('replica', 'fsdp'), 'tensor'), may hold values from -0.25 to 0.25
- error_in: float32 [4, 8192, 8192], P('replica', 'fsdp', 'tensor'), may hold values from -4 to 4
- factor_in: float32 [8192, 32], P('tensor'), may hold values from -0.0625 to 0.0625
Outputs:
- new_error: float32 [4, 8192, 8192], P('replica', 'fsdp', 'tensor')
- update: bfloat16 [8192, 8192], P('fsdp', 'tensor')
- new_factor: float32 [8192, 32], P('tensor')
All inputs are finite; a program needn't handle non-finite values.
Results may differ from a plain program's by a relative error of at most 0.001.
Values may be sent and summed in bfloat16 or wider, within the bound.
A program may use at most 128 MiB of HBM per device.

v0:
```python
import jax
import jax.numpy as jnp
from jax import lax
from jax.sharding import PartitionSpec as P


def fold_rows(out_grad, activations, memory):
    return memory + lax.dot_general(
        activations,
        lax.all_gather(out_grad, "fsdp", axis=0, tiled=True),
        (((0,), (0,)), ((), ())),
        preferred_element_type=jnp.float32,
    )


def orthonormalize(partial_left, replicas):
    left = lax.psum(partial_left, ("replica", "tensor")) / replicas
    gram_local = jnp.dot(left.T, left, precision=lax.Precision.HIGHEST)
    gram_matrix = lax.psum(gram_local, "fsdp")
    triangle = jnp.linalg.cholesky(gram_matrix)
    return jax.scipy.linalg.solve_triangular(triangle, left.T, lower=True).T


def body(attn_out, out_grad, error_in, factor_in):
    activations = lax.all_gather(attn_out, "tensor", axis=0, tiled=True)
    replicas = lax.axis_size("replica")
    projected = jnp.dot(out_grad.astype(jnp.float32), factor_in, precision=lax.Precision.HIGHEST)
    projected_all = lax.all_gather(projected, "fsdp", axis=0, tiled=True)
    partial_left = lax.dot_general(
        activations,
        projected_all,
        (((0,), (0,)), ((), ())),
        precision=lax.Precision.HIGHEST,
        preferred_element_type=jnp.float32,
    )
    partial_left = partial_left + jnp.dot(error_in[0], factor_in, precision=lax.Precision.HIGHEST)
    orthonormal = orthonormalize(partial_left, replicas)
    merged = fold_rows(out_grad, activations, error_in[0])
    factor_local = lax.dot_general(
        merged, orthonormal, (((0,), (0,)), ((), ())), precision=lax.Precision.HIGHEST
    )
    new_factor = lax.psum(factor_local, ("replica", "fsdp")) / replicas
    decompressed = jnp.dot(orthonormal, new_factor.T, precision=lax.Precision.HIGHEST)
    new_error = (merged - decompressed)[None]
    return (new_error, decompressed.astype(jnp.bfloat16), new_factor)


def solution(mesh):
    placed = (
        P(("replica", "tensor"), "fsdp"),
        P(("replica", "fsdp"), "tensor"),
        P("replica", "fsdp", "tensor"),
        P("tensor", None),
    )
    return jax.shard_map(
        body,
        mesh=mesh,
        in_specs=placed,
        out_specs=(P("replica", "fsdp", "tensor"), P("fsdp", "tensor"), P("tensor", None)),
        check_vma=False,
    )
```

profile of v0, /device:TPU:0, one launch (start us, length us, event | category | flops | bytes accessed | tf_op | source)
XLA Modules:
  0.0 355.7 jit_solution(17522907834601763414)
XLA Ops:
  7.2 0.0 copy-start
  7.2 0.0 all-gather.3.cloned.1.call-start
  7.2 0.7 all-gather.3.cloned.1.call-update
  7.9 0.0 all-gather.5.cloned.1.call-start
  8.0 0.7 all-gather.5.cloned.1.call-update
  8.7 0.0 all-reduce.3.cloned.1.call-start
  8.7 0.0 copy-done
  8.7 2.2 fusion.15
  10.9 2.1 all_gather.11
  13.0 34.1 %fusion = f32[4096,32]{0,1:T(8,128)S(1)} fusion(f32[2048,32]{0,1:T(8,128)S(1)} %copy-done, f32[1,4096,2048]{2,1,0:T(8,128)} %param.6), kind=kOutput, calls=%fused_computation | convolution fusion | flops 3221225472 | bytes 34340864 | tf_op jit(solution)/shard_map/dot_general | solution.py:36
  47.2 45.9 %all-gather.3.cloned.1.call-done = bf16[512,4096]{1,0:T(8,128)(2,1)} async-done(((bf16[128,4096]{1,0:T(8,128)(2,1)}), bf16[512,4096]{1,0:T(8,128)(2,1)}) %all-gather.3.cloned.1.call-update) | async-done | bytes 4194320 | tf_op jit(solution)/shard_map/all_gather | solution.py:25
  93.1 5.2 %fusion.2 = f32[4096,32]{0,1:T(8,128)} fusion(f32[4096,32]{0,1:T(8,128)S(1)} %fusion, f32[512,32]{1,0:T(8,128)S(1)} %all_gather.11, bf16[512,4096]{1,0:T(8,128)(2,1)} %all-gather.3.cloned.1.call-done), kind=kOutput, calls=%fused_computation.5 | convolution fusion | flops 805437440 | bytes 5308416 | tf_op jit(solution)/shard_map/dot_general | solution.py:29
  98.3 0.0 all-reduce.3.cloned.1.call-update
  98.3 0.2 all-reduce.5.cloned.1.call-start
  98.5 5.2 %all-gather.5.cloned.1.call-done = bf16[512,2048]{1,0:T(8,128)(2,1)} async-done(((bf16[256,2048]{1,0:T(8,128)(2,1)}), bf16[512,2048]{1,0:T(8,128)(2,1)}) %all-gather.5.cloned.1.call-update) | async-done | bytes 2097168 | tf_op jit(solution)/shard_map/all_gather | solution.py:10
  103.7 28.3 %bitcast_add_fusion = f32[4096,2048]{1,0:T(8,128)} fusion(f32[1,4096,2048]{2,1,0:T(8,128)} %param.6, bf16[512,4096]{1,0:T(8,128)(2,1)} %all-gather.3.cloned.1.call-done, bf16[512,2048]{1,0:T(8,128)(2,1)} %all-gather.5.cloned.1.call-done), kind=kOutput, calls=%fused_computation.2 | convolution fusion | flops 8598323200 | bytes 73400320 | tf_op jit(solution)/shard_map/dot_general | solution.py:8
  132.0 87.7 %all-reduce.3.cloned.1.call-done = f32[4096,32]{0,1:T(8,128)} async-done(((f32[4096,32]{0,1:T(8,128)}), f32[4096,32]{0,1:T(8,128)}) %all-reduce.3.cloned.1.call-update) | async-done | bytes 524304 | tf_op jit(solution)/shard_map/psum | solution.py:17
  219.7 1.8 fusion.5
  221.6 3.4 psum.22
  224.9 0.1 copy.8
  225.0 2.9 cholesky.16
  228.0 0.6 compare_reduce_fusion
  228.6 0.7 fusion.9
  229.3 2.4 custom-call.7
  231.7 1.7 fusion.3
  233.4 24.4 %fusion.16 = f32[2048,32]{0,1:T(8,128)} fusion(f32[4096,2048]{1,0:T(8,128)} %bitcast_add_fusion, f32[32,4096]{1,0:T(8,128)S(1)} %fusion.3), kind=kOutput, calls=%fused_computation.26 | convolution fusion | flops 3221225472 | bytes 34340864 | tf_op jit(solution)/shard_map/dot_general | solution.py:39
  257.8 0.0 all-reduce.5.cloned.1.call-update
  257.8 53.0 %all-reduce.5.cloned.1.call-done = f32[2048,32]{0,1:T(8,128)} async-done(((f32[2048,32]{0,1:T(8,128)}), f32[2048,32]{0,1:T(8,128)}) %all-reduce.5.cloned.1.call-update) | async-done | bytes 262160 | tf_op jit(solution)/shard_map/psum | solution.py:42
  310.8 0.0 copy-start.1
  310.8 1.0 broadcast_multiply_fusion
  311.9 0.0 copy-start.2
  311.9 37.2 %fusion.14 = (bf16[4096,2048]{1,0:T(8,128)(2,1)}, f32[1,4096,2048]{2,1,0:T(8,128)}) fusion(f32[4096,2048]{1,0:T(8,128)} %bitcast_add_fusion, f32[32,4096]{1,0:T(8,128)S(1)} %fusion.3, f32[2048,32]{0,1:T(8,128)S(1)} %broadcast_multiply_fusion), kind=kOutput, calls=%fused_computation.24 | convolution fusion | flops 3238002688 | bytes 84672512 | tf_op jit(solution)/shard_map/dot_general | solution.py:43
  349.1 0.0 copy-done.2
  349.1 0.0 copy-done.1
  (2 shorter events, 0.0 us)
Async XLA Ops:
  7.2 1.5 copy-start
  7.2 85.9 %all-gather.3.cloned.1.call-start = ((), (), s32[]{:S(2)}) async-start(), calls=%async_computation | async-start | bytes 5242880 | tf_op jit(solution)/shard_map/all_gather | solution.py:25
  7.9 95.8 %all-gather.5.cloned.1.call-start = ((), (), s32[]{:S(2)}) async-start(), calls=%async_computation.1 | async-start | bytes 3145728 | tf_op jit(solution)/shard_map/all_gather | solution.py:10
  8.7 211.1 %all-reduce.3.cloned.1.call-start = ((), (), s32[]{:S(2)}) async-start(), calls=%async_computation.2 | async-start | bytes 1048576 | tf_op jit(solution)/shard_map/psum | solution.py:17
  98.3 212.5 %all-reduce.5.cloned.1.call-start = ((), (), s32[]{:S(2)}) async-start(), calls=%async_computation.3 | async-start | bytes 524288 | tf_op jit(solution)/shard_map/psum | solution.py:42
  310.8 38.3 %copy-start.1 = (f32[2048,32]{0,1:T(8,128)S(1)}, f32[2048,32]{0,1:T(8,128)}, u32[]{:S(2)}) copy-start(f32[2048,32]{0,1:T(8,128)} %param.7) | copy-start | bytes 786436
  311.9 37.3 %copy-start.2 = (f32[2048,32]{0,1:T(8,128)}, f32[2048,32]{0,1:T(8,128)S(1)}, u32[]{:S(2)}) copy-start(f32[2048,32]{0,1:T(8,128)S(1)} %broadcast_multiply_fusion) | copy-start | bytes 786436
Sparse Core Ops, SparseCore 0:
  9.6 83.4 all-gather.2
  94.6 9.0 all-gather.4
  109.4 110.2 all-reduce.2
  257.9 52.8 all-reduce.4
where the time goes:
time: 356 us
  waiting for transfers between devices  193 us (54%)
  matrix products  135 us (38%)
  between operations  13.8 us (4%)
  other arithmetic  7.7 us (2%)
  blocking collectives  5.48 us (2%)
    psum x1, waiting for transfers between devices, orthonormalize(): left = lax.psum(partial_left, ('replica', 'tensor')) / replicas  87.7 us
    psum x1, waiting for transfers between devices, body(): new_factor = lax.psum(factor_local, ('replica', 'fsdp')) / replicas  53 us
    all_gather x1, waiting for transfers between devices, body(): activations = lax.all_gather(attn_out, 'tensor', axis=0, tiled=True)  45.9 us
    dot_general x1, matrix products, body(): jnp.dot(orthonormal, new_factor.T, precision=lax.Precision.HIGHEST)  37.2 us
    dot_general x1, matrix products, body(): jnp.dot(error_in[0], factor_in, precision=lax.Precision.HIGHEST)  34.1 us
    dot_general x1, matrix products, fold_rows(): lax.dot_general(activations, lax.all_gather(out_grad, 'fsdp', axis=0, til...  28.3 us
    dot_general x1, matrix products, body(): lax.dot_general(merged, orthonormal, (((0,), (0,)), ((), ())), precision=...  24.4 us
  transfers between devices with their start and end apart: 4, of which 4 were waited for; matrix products, arithmetic and copies ran while one was open for 20% of the time, Pallas kernels for 0%

commit v1 on v0

v1 whole, which is shorter than its diff:
```python
import functools

import jax
import jax.numpy as jnp
from jax import lax
from jax.experimental import pallas as pl
from jax.experimental.pallas import tpu as pltpu
from jax.sharding import PartitionSpec as P

MESH = pl.DeviceIdType.MESH
HIGHEST = lax.Precision.HIGHEST
F32, BF16 = jnp.float32, jnp.bfloat16
LANE = 128
NN = (((1,), (0,)), ((), ()))
NT = (((1,), (1,)), ((), ()))
TN = (((0,), (0,)), ((), ()))
VMEM_BYTES = 60 * 1024 * 1024


def mul(a, b, dims=NN, precision=None):
    return lax.dot_general(a, b, dims, precision=precision, preferred_element_type=F32)


def split(x):
    high = x.astype(BF16)
    return high, (x - high.astype(F32)).astype(BF16)


def stacked(x):
    return jnp.concatenate(split(x), axis=0)


def folded(x):
    half = x.shape[0] // 2
    return x[:half] + x[half:]


class Cut:
    def __init__(self, rows, columns, pieces):
        self.down = 1
        while (columns * self.down) % (pieces * LANE) != 0:
            self.down *= 2
        self.across = pieces // self.down
        self.rows, self.columns = rows // self.down, columns // self.across

    def at(self, piece, start=0):
        row = pl.multiple_of((piece // self.across) * self.rows, 8)
        column = pl.multiple_of(start + (piece % self.across) * self.columns, LANE)
        return pl.ds(row, self.rows), pl.ds(column, self.columns)


def inverse_factor(gram):
    rank = gram.shape[0]
    row_at = lax.broadcasted_iota(jnp.int32, (rank, LANE), 0)
    lane_at = lax.broadcasted_iota(jnp.int32, (rank, LANE), 1)
    table = gram + jnp.where(lane_at == row_at + LANE // 2, 1.0, 0.0).astype(F32)
    for k in range(rank):
        row = table[k : k + 1, :]
        inverse = 1.0 / jnp.sqrt(row[:, k : k + 1])
        row = row * inverse
        column = jnp.where(row_at > k, table[:, k : k + 1] * inverse, 0.0)
        table = jnp.where(row_at == k, jnp.broadcast_to(row, table.shape), table - column * row)
    return table[:, LANE // 2 : LANE // 2 + rank]


def front(
    sizes,
    a_ref, g_ref, f_ref, e_ref,
    q_ref, n_ref, nt_ref,
    e_mem, f_mem, part, left, got_rep, mid, got_ten, gf_slots, gf_all, mix_slots, al_all,
    n_part, n_got, n_full,
    e_sem, gf_sem, rep_sem, ten_sem, ten_back, rep_back, mix_sem, n_sem, n_back,
):
    reps, fs, ts = sizes
    r, f, t = lax.axis_index("replica"), lax.axis_index("fsdp"), lax.axis_index("tensor")
    rank, rows = part.shape
    block = rows // reps
    tile = min(256, block)
    per = block // tile
    tok_g, tok_a = g_ref.shape[0], a_ref.shape[0]

    def row_copy(step):
        q = lax.rem(r + 1 + step // per, reps)
        at = pl.ds(pl.multiple_of(q * block + (step % per) * tile, tile), tile)
        return pltpu.make_async_copy(e_ref.at[at], e_mem.at[at], e_sem.at[step])

    for step in range(reps * per):
        row_copy(step).start()

    plane = [(df, dt) for df in range(fs) for dt in range(ts) if df + dt > 0]
    sheet = [(dr, df) for dr in range(reps) for df in range(fs) if dr + df > 0]

    def in_plane(df, dt):
        return {"replica": r, "fsdp": lax.rem(f + df, fs), "tensor": lax.rem(t + dt, ts)}

    def in_sheet(dr, df):
        return {"replica": lax.rem(r + dr, reps), "fsdp": lax.rem(f + df, fs), "tensor": t}

    barrier = pltpu.get_barrier_semaphore()
    greeted = [in_plane(*d) for d in plane] + [in_sheet(*d) for d in sheet if d[0] > 0]
    for device in greeted:
        pl.semaphore_signal(barrier, inc=1, device_id=device, device_id_type=MESH)

    high, low = split(f_ref[...])
    f_mem[...] = jnp.zeros(f_mem.shape, BF16)
    f_mem[:, 0:rank] = high
    f_mem[:, LANE : LANE + rank] = low

    me_plane = f * ts + t
    projected = mul(g_ref[...], f_mem[...])
    projected = (projected[:, :LANE] + projected[:, LANE:]).T[:rank]
    gf_slots[me_plane] = projected
    pl.semaphore_wait(barrier, len(greeted))

    def spread(slots, sems):
        copies = []
        for i, d in enumerate(plane):
            copies.append(pltpu.make_async_remote_copy(
                src_ref=slots.at[me_plane], dst_ref=slots.at[me_plane],
                send_sem=sems.at[0, i], recv_sem=sems.at[1, i],
                device_id=in_plane(*d), device_id_type=MESH,
            ))
            copies[-1].start()
        return copies

    gf_copies = spread(gf_slots, gf_sem)

    rep_copies = []
    for dr in range(1, reps + 1):
        q = lax.rem(r + dr, reps)
        base = pl.multiple_of(q * block, LANE)

        def tile_left(j, _, dr=dr, base=base):
            row_copy((dr - 1) * per + j).wait()
            at = pl.ds(pl.multiple_of(base + j * tile, tile), tile)
            eh, el = split(e_mem[at, :])
            wide = mul(eh, f_mem[...])
            total = wide[:, :LANE] + wide[:, LANE:] + mul(el, f_mem[:, :LANE])
            part[:, at] = total.T[:rank]
            return 0

        lax.fori_loop(0, per, tile_left, 0)
        if dr == 1:
            for copy in gf_copies:
                copy.wait()
            for df in range(fs):
                total = gf_slots[df * ts]
                for dt in range(1, ts):
                    total = total + gf_slots[df * ts + dt]
                gf_all[:, df * tok_g : (df + 1) * tok_g] = total
        own = stacked(gf_all[:, pl.ds(pl.multiple_of(t * tok_a, LANE), tok_a)])
        at = pl.ds(base, block)
        part[:, at] += folded(mul(own, a_ref[:, at]))
        if dr < reps:
            copy = pltpu.make_async_remote_copy(
                src_ref=part.at[:, at], dst_ref=got_rep.at[dr - 1],
                send_sem=rep_sem.at[0, dr - 1], recv_sem=rep_sem.at[1, dr - 1],
                device_id=in_sheet(dr, 0), device_id_type=MESH,
            )
            copy.start()
            rep_copies.append(copy)

    mine = pl.ds(pl.multiple_of(r * block, LANE), block)
    total = part[:, mine]
    for i, copy in enumerate(rep_copies):
        copy.wait()
        total = total + got_rep[i]
    mid[...] = total

    cut = Cut(rank, block, ts)
    ten_copies = []
    for dt in range(1, ts):
        copy = pltpu.make_async_remote_copy(
            src_ref=mid.at[cut.at(lax.rem(t + dt, ts))], dst_ref=got_ten.at[dt - 1],
            send_sem=ten_sem.at[0, dt - 1], recv_sem=ten_sem.at[1, dt - 1],
            device_id=in_plane(0, dt), device_id_type=MESH,
        )
        copy.start()
        ten_copies.append(copy)
    total = mid[cut.at(t)]
    for i, copy in enumerate(ten_copies):
        copy.wait()
        total = total + got_ten[i]
    own = cut.at(t, r * block)
    left[own] = total * (1.0 / reps)
    back = []
    for dt in range(1, ts):
        copy = pltpu.make_async_remote_copy(
            src_ref=left.at[own], dst_ref=left.at[own],
            send_sem=ten_back.at[0, dt - 1], recv_sem=ten_back.at[1, dt - 1],
            device_id=in_plane(0, dt), device_id_type=MESH,
        )
        copy.start()
        back.append(copy)
    for copy in back:
        copy.wait()
    back = []
    for dr in range(1, reps):
        copy = pltpu.make_async_remote_copy(
            src_ref=left.at[:, mine], dst_ref=left.at[:, mine],
            send_sem=rep_back.at[0, dr - 1], recv_sem=rep_back.at[1, dr - 1],
            device_id=in_sheet(dr, 0), device_id_type=MESH,
        )
        copy.start()
        back.append(copy)
    for copy in back:
        copy.wait()

    whole = left[...]
    mix_slots[me_plane, :, 0:LANE] = jnp.zeros((rank, LANE), F32)
    mix_slots[me_plane, :, 0:rank] = mul(whole, whole, NT, HIGHEST)
    mix_slots[me_plane, :, LANE:] = folded(mul(stacked(whole), a_ref[...], NT))
    mix_copies = spread(mix_slots, mix_sem)

    n_part[...] = jnp.zeros(n_part.shape, F32)

    def tile_right(j, _):
        at = pl.ds(pl.multiple_of(j * tile, tile), tile)
        eh, el = split(e_mem[at, :])
        both = stacked(left[:, at])
        n_part[...] += folded(mul(both, eh)) + mul(both[:rank], el)
        return 0

    lax.fori_loop(0, rows // tile, tile_right, 0)

    for copy in mix_copies:
        copy.wait()
    for dt in range(ts):
        total = mix_slots[dt, :, LANE:]
        for df in range(1, fs):
            total = total + mix_slots[df * ts + dt, :, LANE:]
        al_all[:, dt * tok_a : (dt + 1) * tok_a] = total
    tokens = stacked(al_all[:, pl.ds(pl.multiple_of(f * tok_g, LANE), tok_g)])
    n_part[...] += folded(mul(tokens, g_ref[...]))

    n_cut = Cut(rank, n_part.shape[1], reps * fs)
    n_copies = []
    for i, (dr, df) in enumerate(sheet):
        owner = lax.rem(r + dr, reps) * fs + lax.rem(f + df, fs)
        copy = pltpu.make_async_remote_copy(
            src_ref=n_part.at[n_cut.at(owner)], dst_ref=n_got.at[i],
            send_sem=n_sem.at[0, i], recv_sem=n_sem.at[1, i],
            device_id=in_sheet(dr, df), device_id_type=MESH,
        )
        copy.start()
        n_copies.append(copy)

    gram = mix_slots[0, :, 0:LANE]
    for df in range(1, fs):
        gram = gram + mix_slots[df * ts, :, 0:LANE]
    inverse = inverse_factor(gram)
    high, low = split(mul(inverse, left[...], precision=HIGHEST))
    q_ref[0:rank] = high
    q_ref[rank : 2 * rank] = low
    q_ref[2 * rank :] = high

    place = n_cut.at(r * fs + f)
    total = n_part[place]
    for i, copy in enumerate(n_copies):
        copy.wait()
        total = total + n_got[i]
    n_full[place] = total * (1.0 / reps)
    back = []
    for i, (dr, df) in enumerate(sheet):
        copy = pltpu.make_async_remote_copy(
            src_ref=n_full.at[place], dst_ref=n_full.at[place],
            send_sem=n_back.at[0, i], recv_sem=n_back.at[1, i],
            device_id=in_sheet(dr, df), device_id_type=MESH,
        )
        copy.start()
        back.append(copy)
    for copy in back:
        copy.wait()
    factor = mul(inverse, n_full[...], precision=HIGHEST)
    n_ref[...] = factor
    high, low = split(factor)
    nt_ref[0:rank] = high
    nt_ref[rank : 2 * rank] = high
    nt_ref[2 * rank :] = low


def run_front(sizes, a, g, f, e):
    reps, fs, ts = sizes
    rank, rows, columns = f.shape[1], e.shape[0], e.shape[1]
    tok_g, tok_a = g.shape[0], a.shape[0]
    block = rows // reps
    cut, n_cut = Cut(rank, block, ts), Cut(rank, columns, reps * fs)
    tiles = rows // min(256, block)
    plane, sheet = fs * ts - 1, reps * fs - 1
    vmem = pl.BlockSpec(memory_space=pltpu.VMEM)
    dma = pltpu.SemaphoreType.DMA
    return pl.pallas_call(
        functools.partial(front, sizes),
        out_shape=(
            jax.ShapeDtypeStruct((3 * rank, rows), BF16),
            jax.ShapeDtypeStruct((rank, columns), F32),
            jax.ShapeDtypeStruct((3 * rank, columns), BF16),
        ),
        in_specs=[vmem, vmem, vmem, pl.BlockSpec(memory_space=pl.ANY)],
        out_specs=(vmem, vmem, vmem),
        scratch_shapes=[
            pltpu.VMEM((rows, columns), F32),
            pltpu.VMEM((columns, 2 * LANE), BF16),
            pltpu.VMEM((rank, rows), F32),
            pltpu.VMEM((rank, rows), F32),
            pltpu.VMEM((reps - 1, rank, block), F32),
            pltpu.VMEM((rank, block), F32),
            pltpu.VMEM((ts - 1, cut.rows, cut.columns), F32),
            pltpu.VMEM((fs * ts, rank, tok_g), F32),
            pltpu.VMEM((rank, tok_g * fs), F32),
            pltpu.VMEM((fs * ts, rank, LANE + tok_a), F32),
            pltpu.VMEM((rank, tok_a * ts), F32),
            pltpu.VMEM((rank, columns), F32),
            pltpu.VMEM((sheet, n_cut.rows, n_cut.columns), F32),
            pltpu.VMEM((rank, columns), F32),
            dma((tiles,)), dma((2, plane)), dma((2, reps - 1)), dma((2, ts - 1)), dma((2, ts - 1)),
            dma((2, reps - 1)), dma((2, plane)), dma((2, sheet)), dma((2, sheet)),
        ],
        compiler_params=pltpu.CompilerParams(
            collective_id=0, has_side_effects=True, vmem_limit_bytes=VMEM_BYTES
        ),
        cost_estimate=pl.CostEstimate(
            flops=100_000_000_000, bytes_accessed=rows * columns * 8, transcendentals=0
        ),
        name="front",
    )(a, g, f, e)


def finish(a_ref, g_ref, e_ref, q_ref, n_ref, error_ref, update_ref):
    low_rank = mul(q_ref[...], n_ref[...], TN)
    grad = mul(a_ref[...], g_ref[...], TN)
    error_ref[...] = grad + e_ref[...] - low_rank
    update_ref[...] = low_rank.astype(BF16)


def run_finish(a, g, e, q, n):
    rows, columns = e.shape
    tile = min(256, rows)

    def whole(x):
        return pl.BlockSpec(x.shape, lambda i: (0, 0))

    def tall(x):
        return pl.BlockSpec((x.shape[0], tile), lambda i: (0, i))

    flat = pl.BlockSpec((tile, columns), lambda i: (i, 0))
    return pl.pallas_call(
        finish,
        out_shape=(jax.ShapeDtypeStruct(e.shape, F32), jax.ShapeDtypeStruct(e.shape, BF16)),
        grid=(rows // tile,),
        in_specs=[tall(a), whole(g), flat, tall(q), whole(n)],
        out_specs=(flat, flat),
        compiler_params=pltpu.CompilerParams(vmem_limit_bytes=VMEM_BYTES),
        name="finish",
    )(a, g, e, q, n)


def solution(mesh):
    sizes = (mesh.shape["replica"], mesh.shape["fsdp"], mesh.shape["tensor"])

    def body(attn_out, out_grad, error_in, factor_in):
        memory = error_in[0]
        activations = lax.all_gather(attn_out, "tensor", axis=0, tiled=True)
        cotangents = lax.all_gather(out_grad, "fsdp", axis=0, tiled=True)
        q, factor, n = run_front(sizes, attn_out, out_grad, factor_in, memory)
        new_error, update = run_finish(activations, cotangents, memory, q, n)
        return new_error[None], update, factor.T

    placed = (
        P(("replica", "tensor"), "fsdp"),
        P(("replica", "fsdp"), "tensor"),
        P("replica", "fsdp", "tensor"),
        P("tensor", None),
    )
    return jax.shard_map(
        body,
        mesh=mesh,
        in_specs=placed,
        out_specs=(P("replica", "fsdp", "tensor"), P("fsdp", "tensor"), P("tensor", None)),
        check_vma=False,
    )
```

time: 356 us -> 162 us (0.46)
  waiting for transfers between devices: 193 us -> 33.1 us
  matrix products: 135 us -> 0 us
  Pallas kernels: 0 us -> 111 us
  other arithmetic: 7.7 us -> 0 us
  blocking collectives: 5.48 us -> 0 us
    psum x2 -> x0, waiting for transfers between devices: 141 us -> none  [the longest x1 87.7 us: orthonormalize(): left = lax.psum(partial_left, ('replica', 'tensor')) / replicas]
    dot_general x7 -> x0, matrix products: 133 us -> none  [the longest x1 37.2 us: body(): jnp.dot(orthonormal, new_factor.T, precision=lax.Precision.HIGHEST)]
    pallas_call x0 -> x2, Pallas kernels: none -> 111 us  [the longest x1 74.5 us: run_front(): pl.pallas_call(functools.partial(front, sizes), out_shape=(jax.ShapeDtype...]
    all_gather x1, waiting for transfers between devices: 45.9 us -> 31.7 us  [body(): activations = lax.all_gather(attn_out, 'tensor', axis=0, tiled=True)]
    another operation x5 -> x0, other arithmetic: 6.68 us -> none  [the longest x3 3.59 us: orthonormalize(): triangle = jnp.linalg.cholesky(gram_matrix)]
    all_gather x1, waiting for transfers between devices: 5.16 us -> 0.02 us  [body(): cotangents = lax.all_gather(out_grad, 'fsdp', axis=0, tiled=True)]
  transfers between devices with their start and end apart: 4 -> 2, of which waited for: 4 -> 1; matrix products, arithmetic and copies ran while one was open for 20% -> 1% of each run, Pallas kernels for 0% -> 46%
where the time goes in v1:
time: 162 us
  Pallas kernels  111 us (69%)
  waiting for transfers between devices  33.1 us (20%)
  between operations  14.1 us (9%)
  local copies, waits for them, and re-layouts  2.97 us (2%)
    pallas_call x1, Pallas kernels, run_front(): pl.pallas_call(functools.partial(front, sizes), out_shape=(jax.ShapeDtype...  74.5 us
    pallas_call x1, Pallas kernels, run_finish(): pl.pallas_call(finish, out_shape=(jax.ShapeDtypeStruct(e.shape, F32), jax...  36.9 us
    all_gather x1, waiting for transfers between devices, body(): activations = lax.all_gather(attn_out, 'tensor', axis=0, tiled=True)  31.7 us
  transfers between devices with their start and end apart: 2, of which 1 were waited for; matrix products, arithmetic and copies ran while one was open for 1% of the time, Pallas kernels for 46%

profile of v1, /device:TPU:0, one launch (start us, length us, event | category | flops | bytes accessed | tf_op | source)
XLA Modules:
  0.0 161.5 jit_solution(1796060587912173458)
XLA Ops:
  7.2 0.0 all-gather.5.cloned.1.call-start
  7.2 0.7 all-gather.5.cloned.1.call-update
  7.9 0.0 all-gather.3.cloned.1.call-start
  7.9 0.7 all-gather.3.cloned.1.call-update
  8.6 2.3 %copy.7.f_ref = f32[2048,32]{1,0:T(8,128)} copy(f32[2048,32]{0,1:T(8,128)} %param.7) | data formatting | bytes 524288 | tf_op args[3]
  10.9 74.5 %front.1 = (bf16[96,4096]{1,0:T(8,128)(2,1)}, f32[32,2048]{1,0:T(8,128)}, bf16[96,2048]{1,0:T(8,128)(2,1)}) custom-call(bf16[128,4096]{1,0:T(8,128)(2,1)} %a_ref.1, bf16[256,2048]{1,0:T(8,128)(2,1)} %g_ref.1, f32[2048,32]{1,0:T(8,128)} %copy.7.f_ref, f32[4096,2048]{1,0:T(8,128)} %bitcast.3), custom_call_target="tpu_custom_call" | custom-call | flops 99999997952 | bytes 67108864 | tf_op jit(solution)/shard_map/front/pallas_call | solution.py:292
  85.4 0.0 all-gather.5.cloned.1.call-done.g_ref
  85.4 31.7 %all-gather.3.cloned.1.call-done.a_ref = bf16[512,4096]{1,0:T(8,128)(2,1)} async-done(((bf16[128,4096]{1,0:T(8,128)(2,1)}), bf16[512,4096]{1,0:T(8,128)(2,1)}) %all-gather.3.cloned.1.call-update) | async-done | bytes 4194320 | tf_op jit(solution)/shard_map/all_gather | solution.py:363
  117.1 0.0 copy-start
  117.1 36.9 %finish.1 = (f32[4096,2048]{1,0:T(8,128)}, bf16[4096,2048]{1,0:T(8,128)(2,1)}) custom-call(bf16[512,4096]{1,0:T(8,128)(2,1)} %all-gather.3.cloned.1.call-done.a_ref, bf16[512,2048]{1,0:T(8,128)(2,1)} %all-gather.5.cloned.1.call-done.g_ref, f32[4096,2048]{1,0:T(8,128)} %bitcast.4, bf16[96,4096]{1,0:T(8,128)(2,1)} %get-tuple-element.8.q_ref, ...), custom_call_target="tpu_custom_call" | custom-call | tf_op jit(solution)/shard_map/finish/pallas_call | solution.py:347
  154.0 0.0 copy-done
  154.0 0.7 copy.9
Async XLA Ops:
  7.2 78.2 %all-gather.5.cloned.1.call-start = ((), (), s32[]{:S(2)}) async-start(), calls=%async_computation.1 | async-start | bytes 3145728 | tf_op jit(solution)/shard_map/all_gather | solution.py:364
  7.9 109.2 %all-gather.3.cloned.1.call-start = ((), (), s32[]{:S(2)}) async-start(), calls=%async_computation | async-start | bytes 5242880 | tf_op jit(solution)/shard_map/all_gather | solution.py:363
  117.1 36.9 %copy-start = (f32[32,2048]{1,0:T(8,128)S(1)}, f32[32,2048]{1,0:T(8,128)}, u32[]{:S(2)}) copy-start(f32[32,2048]{1,0:T(8,128)} %get-tuple-element.12) | copy-start | bytes 786436
Sparse Core Ops, SparseCore 0:
  9.5 13.2 all-gather.4
  24.4 92.6 all-gather.2

commit v2 on v1

--- a/solution.py
+++ b/solution.py
@@ -14,7 +14,7 @@
 NN = (((1,), (0,)), ((), ()))
 NT = (((1,), (1,)), ((), ()))
 TN = (((0,), (0,)), ((), ()))
-VMEM_BYTES = 60 * 1024 * 1024
+VMEM_BYTES = 20 * 1024 * 1024
 
 
 def mul(a, b, dims=NN, precision=None):
@@ -66,10 +66,10 @@
 def front(
     sizes,
     a_ref, g_ref, f_ref, e_ref,
-    q_ref, n_ref, nt_ref,
-    e_mem, f_mem, part, left, got_rep, mid, got_ten, gf_slots, gf_all, mix_slots, al_all,
+    q_ref, n_ref, nt_ref, e_mem, a_all, g_all,
+    f_mem, part, left, got_rep, mid, got_ten, gf_slots, gf_all, mix_slots, al_all,
     n_part, n_got, n_full,
-    e_sem, gf_sem, rep_sem, ten_sem, ten_back, rep_back, mix_sem, n_sem, n_back,
+    e_sem, own_sem, ring_sem, g_sem, gf_sem, rep_sem, ten_sem, ten_back, rep_back, mix_sem, n_sem, n_back,
 ):
     reps, fs, ts = sizes
     r, f, t = lax.axis_index("replica"), lax.axis_index("fsdp"), lax.axis_index("tensor")
@@ -102,14 +102,13 @@
         pl.semaphore_signal(barrier, inc=1, device_id=device, device_id_type=MESH)
 
     high, low = split(f_ref[...])
-    f_mem[...] = jnp.zeros(f_mem.shape, BF16)
-    f_mem[:, 0:rank] = high
-    f_mem[:, LANE : LANE + rank] = low
+    wide = jnp.concatenate(
+        [high.astype(F32), low.astype(F32), jnp.zeros((LANE - 2 * rank, f_ref.shape[1]), F32)], axis=0
+    )
+    f_mem[...] = wide.T.astype(BF16)
 
     me_plane = f * ts + t
-    projected = mul(g_ref[...], f_mem[...])
-    projected = (projected[:, :LANE] + projected[:, LANE:]).T[:rank]
-    gf_slots[me_plane] = projected
+    gf_slots[me_plane] = folded(mul(g_ref[...], f_mem[...]).T[: 2 * rank])
     pl.semaphore_wait(barrier, len(greeted))
 
     def spread(slots, sems):
@@ -125,6 +124,47 @@
 
     gf_copies = spread(gf_slots, gf_sem)
 
+    g_own = pl.ds(pl.multiple_of(f * tok_g, tok_g), tok_g)
+    a_own = pl.ds(pl.multiple_of(t * tok_a, tok_a), tok_a)
+    own_copies = [
+        pltpu.make_async_copy(a_ref, a_all.at[a_own], own_sem.at[0]),
+        pltpu.make_async_copy(g_ref, g_all.at[g_own], own_sem.at[1]),
+    ]
+    for copy in own_copies:
+        copy.start()
+    g_copies = []
+    for df in range(1, fs):
+        copy = pltpu.make_async_remote_copy(
+            src_ref=g_ref, dst_ref=g_all.at[g_own],
+            send_sem=g_sem.at[0, df - 1], recv_sem=g_sem.at[1, df - 1],
+            device_id=in_plane(df, 0), device_id_type=MESH,
+        )
+        copy.start()
+        g_copies.append(copy)
+
+    half = tok_a // 2
+
+    def ring_copy(step, way, part_at):
+        block_at = lax.rem(t - step + ts, ts) if way == 0 else lax.rem(t + step, ts)
+        upper = (part_at == 0) == (way == 0)
+        first = 0 if upper else half
+        rows_at = pl.ds(pl.multiple_of(block_at * tok_a + first, half), half)
+        src = a_ref.at[pl.ds(first, half)] if step == 0 else a_all.at[rows_at]
+        slot = (step * 2 + way) * 2 + part_at
+        return pltpu.make_async_remote_copy(
+            src_ref=src, dst_ref=a_all.at[rows_at],
+            send_sem=ring_sem.at[0, slot], recv_sem=ring_sem.at[1, slot],
+            device_id=in_plane(0, 1 if way == 0 else ts - 1), device_id_type=MESH,
+        )
+
+    hops = ts // 2
+    ring = [
+        [ring_copy(step, way, p) for p in range(2 if 2 * step + 2 < ts else 1) for way in range(2)]
+        for step in range(hops)
+    ]
+    for copy in ring[0]:
+        copy.start()
+
     rep_copies = []
     for dr in range(1, reps + 1):
         q = lax.rem(r + dr, reps)
@@ -134,9 +174,8 @@
             row_copy((dr - 1) * per + j).wait()
             at = pl.ds(pl.multiple_of(base + j * tile, tile), tile)
             eh, el = split(e_mem[at, :])
-            wide = mul(eh, f_mem[...])
-            total = wide[:, :LANE] + wide[:, LANE:] + mul(el, f_mem[:, :LANE])
-            part[:, at] = total.T[:rank]
+            total = mul(eh, f_mem[...]) + mul(el, f_mem[...])
+            part[:, at] = folded(total.T[: 2 * rank])
             return 0
 
         lax.fori_loop(0, per, tile_left, 0)
@@ -160,6 +199,18 @@
             copy.start()
             rep_copies.append(copy)
 
+    ring_waited = set()
+
+    def forward(step):
+        ready = [c for c in ring[step - 1]][: len(ring[step])]
+        for i, copy in enumerate(ready):
+            copy.wait_recv()
+            ring_waited.add((step - 1, i))
+        for copy in ring[step]:
+            copy.start()
+
+    if hops > 1:
+        forward(1)
     mine = pl.ds(pl.multiple_of(r * block, LANE), block)
     total = part[:, mine]
     for i, copy in enumerate(rep_copies):
@@ -271,6 +322,15 @@
         back.append(copy)
     for copy in back:
         copy.wait()
+    for step in range(2, hops):
+        forward(step)
+    for step in range(hops):
+        for i, copy in enumerate(ring[step]):
+            copy.wait_send()
+            if (step, i) not in ring_waited:
+                copy.wait_recv()
+    for copy in own_copies + g_copies:
+        copy.wait()
     factor = mul(inverse, n_full[...], precision=HIGHEST)
     n_ref[...] = factor
     high, low = split(factor)
@@ -281,7 +341,7 @@
 
 def run_front(sizes, a, g, f, e):
     reps, fs, ts = sizes
-    rank, rows, columns = f.shape[1], e.shape[0], e.shape[1]
+    rank, rows, columns = f.shape[0], e.shape[0], e.shape[1]
     tok_g, tok_a = g.shape[0], a.shape[0]
     block = rows // reps
     cut, n_cut = Cut(rank, block, ts), Cut(rank, columns, reps * fs)
@@ -295,12 +355,14 @@
             jax.ShapeDtypeStruct((3 * rank, rows), BF16),
             jax.ShapeDtypeStruct((rank, columns), F32),
             jax.ShapeDtypeStruct((3 * rank, columns), BF16),
+            pltpu.VMEM((rows, columns), F32),
+            pltpu.VMEM((tok_a * ts, rows), BF16),
+            pltpu.VMEM((tok_g * fs, columns), BF16),
         ),
         in_specs=[vmem, vmem, vmem, pl.BlockSpec(memory_space=pl.ANY)],
-        out_specs=(vmem, vmem, vmem),
+        out_specs=(vmem,) * 6,
         scratch_shapes=[
-            pltpu.VMEM((rows, columns), F32),
-            pltpu.VMEM((columns, 2 * LANE), BF16),
+            pltpu.VMEM((columns, LANE), BF16),
             pltpu.VMEM((rank, rows), F32),
             pltpu.VMEM((rank, rows), F32),
             pltpu.VMEM((reps - 1, rank, block), F32),
@@ -313,7 +375,7 @@
             pltpu.VMEM((rank, columns), F32),
             pltpu.VMEM((sheet, n_cut.rows, n_cut.columns), F32),
             pltpu.VMEM((rank, columns), F32),
-            dma((tiles,)), dma((2, plane)), dma((2, reps - 1)), dma((2, ts - 1)), dma((2, ts - 1)),
+            dma((tiles,)), dma((2,)), dma((2, 4 * max(1, ts // 2))), dma((2, max(1, fs - 1))), dma((2, plane)), dma((2, reps - 1)), dma((2, ts - 1)), dma((2, ts - 1)),
             dma((2, reps - 1)), dma((2, plane)), dma((2, sheet)), dma((2, sheet)),
         ],
         compiler_params=pltpu.CompilerParams(
@@ -327,9 +389,11 @@
 
 
 def finish(a_ref, g_ref, e_ref, q_ref, n_ref, error_ref, update_ref):
+    tile = error_ref.shape[0]
+    at = pl.ds(pl.multiple_of(pl.program_id(0) * tile, tile), tile)
     low_rank = mul(q_ref[...], n_ref[...], TN)
-    grad = mul(a_ref[...], g_ref[...], TN)
-    error_ref[...] = grad + e_ref[...] - low_rank
+    grad = mul(a_ref[:, at], g_ref[...], TN)
+    error_ref[...] = grad + e_ref[at, :] - low_rank
     update_ref[...] = low_rank.astype(BF16)
 
 
@@ -344,26 +408,26 @@
         return pl.BlockSpec((x.shape[0], tile), lambda i: (0, i))
 
     flat = pl.BlockSpec((tile, columns), lambda i: (i, 0))
+    vmem = pl.BlockSpec(memory_space=pltpu.VMEM)
     return pl.pallas_call(
         finish,
         out_shape=(jax.ShapeDtypeStruct(e.shape, F32), jax.ShapeDtypeStruct(e.shape, BF16)),
         grid=(rows // tile,),
-        in_specs=[tall(a), whole(g), flat, tall(q), whole(n)],
+        in_specs=[vmem, vmem, vmem, tall(q), whole(n)],
         out_specs=(flat, flat),
         compiler_params=pltpu.CompilerParams(vmem_limit_bytes=VMEM_BYTES),
         name="finish",
-    )(a, g, e, q, n)
+    )(*(pltpu.with_memory_space_constraint(x, pltpu.VMEM) for x in (a, g, e)), q, n)
 
 
 def solution(mesh):
     sizes = (mesh.shape["replica"], mesh.shape["fsdp"], mesh.shape["tensor"])
 
     def body(attn_out, out_grad, error_in, factor_in):
-        memory = error_in[0]
-        activations = lax.all_gather(attn_out, "tensor", axis=0, tiled=True)
-        cotangents = lax.all_gather(out_grad, "fsdp", axis=0, tiled=True)
-        q, factor, n = run_front(sizes, attn_out, out_grad, factor_in, memory)
-        new_error, update = run_finish(activations, cotangents, memory, q, n)
+        q, factor, n, held, activations, cotangents = run_front(
+            sizes, attn_out, out_grad, factor_in.T, error_in[0]
+        )
+        new_error, update = run_finish(activations, cotangents, held, q, n)
         return new_error[None], update, factor.T
 
     placed = (

time: 162 us -> 138 us (0.85)
  waiting for transfers between devices: 33.1 us -> 0 us
  Pallas kernels: 111 us -> 137 us
  between operations: 14.1 us -> 0.65 us
  local copies, waits for them, and re-layouts: 2.97 us -> 0.71 us
    pallas_call x1, Pallas kernels: 74.5 us -> 116 us  [run_front(): pl.pallas_call(functools.partial(front, sizes), out_shape=(jax.ShapeDtype...]
    all_gather x2 -> x0, waiting for transfers between devices: 31.7 us -> none  [the longest x1 31.7 us: body(): activations = lax.all_gather(attn_out, 'tensor', axis=0, tiled=True)]
    pallas_call x1, Pallas kernels: 36.9 us -> 20.8 us  [run_finish(): pl.pallas_call(finish, out_shape=(jax.ShapeDtypeStruct(e.shape, F32), jax...]
    unnamed x4 -> x3, local copies, waits for them, and re-layouts: 2.97 us -> 0.71 us
  transfers between devices with their start and end apart: 2 -> 0, of which waited for: 1 -> 0; matrix products, arithmetic and copies ran while one was open for 1% -> 0% of each run, Pallas kernels for 46% -> 0%
where the time goes in v2:
time: 138 us
  Pallas kernels  137 us (99%)
    pallas_call x1, Pallas kernels, run_front(): pl.pallas_call(functools.partial(front, sizes), out_shape=(jax.ShapeDtype...  116 us
    pallas_call x1, Pallas kernels, run_finish(): pl.pallas_call(finish, out_shape=(jax.ShapeDtypeStruct(e.shape, F32), jax...  20.8 us

profile of v2, /device:TPU:0, one launch (start us, length us, event | category | flops | bytes accessed | tf_op | source)
XLA Modules:
  0.0 137.9 jit_solution(10473600916817677070)
XLA Ops:
  0.6 115.7 %front.1 = (bf16[96,4096]{1,0:T(8,128)(2,1)}, f32[32,2048]{1,0:T(8,128)}, bf16[96,2048]{1,0:T(8,128)(2,1)}, f32[4096,2048]{1,0:T(8,128)S(1)}, bf16[512,4096]{1,0...) custom-call(bf16[128,4096]{1,0:T(8,128)(2,1)} %a_ref.1, bf16[256,2048]{1,0:T(8,128)(2,1)} %g_ref.1, f32[32,2048]{1,0:T(8,128)} %bitcast.7, ...), custom_call_target="tpu_custom_call" | custom-call | flops 99999997952 | bytes 67108864 | tf_op jit(solution)/shard_map/front/pallas_call | solution.py:352
  116.4 0.0 copy-start
  116.4 20.8 %finish.1 = (f32[4096,2048]{1,0:T(8,128)}, bf16[4096,2048]{1,0:T(8,128)(2,1)}) custom-call(bf16[512,4096]{1,0:T(8,128)(2,1)S(1)} %get-tuple-element.11.a_ref, bf16[512,2048]{1,0:T(8,128)(2,1)S(1)} %get-tuple-element.12.g_ref, f32[4096,2048]{1,0:T(8,128)S(1)} %get-tuple-element.13.e_ref, bf16[96,4096]{1,0:T(8,128)(2,1)} %get-tuple-element.14.q_ref, ...), custom_call_target="tpu_custom_call" | custom-call | tf_op jit(solution)/shard_map/finish/pallas_call | solution.py:412
  137.2 0.0 copy-done
  137.2 0.7 copy.8
Async XLA Ops:
  116.4 20.8 %copy-start = (f32[32,2048]{1,0:T(8,128)S(1)}, f32[32,2048]{1,0:T(8,128)}, u32[]{:S(2)}) copy-start(f32[32,2048]{1,0:T(8,128)} %get-tuple-element.18) | copy-start | bytes 786436

commit v3 on v2

--- a/solution.py
+++ b/solution.py
@@ -142,28 +142,63 @@
         copy.start()
         g_copies.append(copy)
 
-    half = tok_a // 2
-
-    def ring_copy(step, way, part_at):
-        block_at = lax.rem(t - step + ts, ts) if way == 0 else lax.rem(t + step, ts)
-        upper = (part_at == 0) == (way == 0)
-        first = 0 if upper else half
-        rows_at = pl.ds(pl.multiple_of(block_at * tok_a + first, half), half)
-        src = a_ref.at[pl.ds(first, half)] if step == 0 else a_all.at[rows_at]
-        slot = (step * 2 + way) * 2 + part_at
-        return pltpu.make_async_remote_copy(
-            src_ref=src, dst_ref=a_all.at[rows_at],
+    pieces = 4
+    piece = tok_a // pieces
+
+    def rows_of(block_at, p):
+        return pl.ds(pl.multiple_of(block_at * tok_a + p * piece, piece), piece)
+
+    def inside(x):
+        return jnp.logical_and(x >= 0, x < ts)
+
+    def bulk(way, d, p):
+        sign = 1 - 2 * way
+        block_at = t if d <= 2 else t - sign * (d - 1)
+        dest = t + sign * (d if d <= 2 else 1)
+        held = lax.rem(block_at + ts, ts)
+        src = a_ref.at[pl.ds(p * piece, piece)] if d <= 2 else a_all.at[rows_of(held, p)]
+        slot = (way * (ts - 1) + d - 1) * pieces + p
+        copy = pltpu.make_async_remote_copy(
+            src_ref=src, dst_ref=a_all.at[rows_of(held, p)],
             send_sem=ring_sem.at[0, slot], recv_sem=ring_sem.at[1, slot],
-            device_id=in_plane(0, 1 if way == 0 else ts - 1), device_id_type=MESH,
-        )
-
-    hops = ts // 2
-    ring = [
-        [ring_copy(step, way, p) for p in range(2 if 2 * step + 2 < ts else 1) for way in range(2)]
-        for step in range(hops)
-    ]
-    for copy in ring[0]:
-        copy.start()
+            device_id={"replica": r, "fsdp": f, "tensor": lax.rem(dest + ts, ts)},
+            device_id_type=MESH,
+        )
+        return copy, jnp.logical_and(inside(block_at), inside(dest))
+
+    started, landed = [], set()
+
+    def send(d, p):
+        if d >= ts:
+            return
+        for way in range(2):
+            copy, valid = bulk(way, d, p)
+            pl.when(valid)(copy.start)
+            started.append((copy, valid))
+
+    def land(d, p):
+        if d >= ts or (d, p) in landed:
+            return
+        landed.add((d, p))
+        for way in range(2):
+            sign = 1 - 2 * way
+            block_at = t - sign * d
+            at = a_all.at[rows_of(lax.rem(block_at + ts, ts), p)]
+            slot = (way * (ts - 1) + d - 1) * pieces + p
+            copy = pltpu.make_async_remote_copy(
+                src_ref=at, dst_ref=at, send_sem=ring_sem.at[0, slot], recv_sem=ring_sem.at[1, slot],
+                device_id=in_plane(0, 1), device_id_type=MESH,
+            )
+            pl.when(inside(block_at))(copy.wait_recv)
+
+    def pass_on(p):
+        if ts > 3:
+            land(2, p)
+            send(3, p)
+
+    send(2, 0)
+    send(2, 1)
+    send(1, 0)
 
     rep_copies = []
     for dr in range(1, reps + 1):
@@ -199,18 +234,6 @@
             copy.start()
             rep_copies.append(copy)
 
-    ring_waited = set()
-
-    def forward(step):
-        ready = [c for c in ring[step - 1]][: len(ring[step])]
-        for i, copy in enumerate(ready):
-            copy.wait_recv()
-            ring_waited.add((step - 1, i))
-        for copy in ring[step]:
-            copy.start()
-
-    if hops > 1:
-        forward(1)
     mine = pl.ds(pl.multiple_of(r * block, LANE), block)
     total = part[:, mine]
     for i, copy in enumerate(rep_copies):
@@ -245,6 +268,9 @@
         back.append(copy)
     for copy in back:
         copy.wait()
+    send(2, 2)
+    pass_on(0)
+    pass_on(1)
     back = []
     for dr in range(1, reps):
         copy = pltpu.make_async_remote_copy(
@@ -262,6 +288,9 @@
     mix_slots[me_plane, :, 0:rank] = mul(whole, whole, NT, HIGHEST)
     mix_slots[me_plane, :, LANE:] = folded(mul(stacked(whole), a_ref[...], NT))
     mix_copies = spread(mix_slots, mix_sem)
+    send(2, 3)
+    for p in range(1, pieces):
+        send(1, p)
 
     n_part[...] = jnp.zeros(n_part.shape, F32)
 
@@ -276,6 +305,7 @@
 
     for copy in mix_copies:
         copy.wait()
+    pass_on(2)
     for dt in range(ts):
         total = mix_slots[dt, :, LANE:]
         for df in range(1, fs):
@@ -322,13 +352,16 @@
         back.append(copy)
     for copy in back:
         copy.wait()
-    for step in range(2, hops):
-        forward(step)
-    for step in range(hops):
-        for i, copy in enumerate(ring[step]):
-            copy.wait_send()
-            if (step, i) not in ring_waited:
-                copy.wait_recv()
+    pass_on(3)
+    for d in range(4, ts):
+        for p in range(pieces):
+            land(d - 1, p)
+            send(d, p)
+    for d in range(1, ts):
+        for p in range(pieces):
+            land(d, p)
+    for copy, valid in started:
+        pl.when(valid)(copy.wait_send)
     for copy in own_copies + g_copies:
         copy.wait()
     factor = mul(inverse, n_full[...], precision=HIGHEST)
@@ -375,7 +408,7 @@
             pltpu.VMEM((rank, columns), F32),
             pltpu.VMEM((sheet, n_cut.rows, n_cut.columns), F32),
             pltpu.VMEM((rank, columns), F32),
-            dma((tiles,)), dma((2,)), dma((2, 4 * max(1, ts // 2))), dma((2, max(1, fs - 1))), dma((2, plane)), dma((2, reps - 1)), dma((2, ts - 1)), dma((2, ts - 1)),
+            dma((tiles,)), dma((2,)), dma((2, 8 * max(1, ts - 1))), dma((2, max(1, fs - 1))), dma((2, plane)), dma((2, reps - 1)), dma((2, ts - 1)), dma((2, ts - 1)),
             dma((2, reps - 1)), dma((2, plane)), dma((2, sheet)), dma((2, sheet)),
         ],
         compiler_params=pltpu.CompilerParams(

time: 138 us -> 129 us (0.935)
  Pallas kernels: 137 us -> 127 us
    pallas_call x1, Pallas kernels: 116 us -> 107 us  [run_front(): pl.pallas_call(functools.partial(front, sizes), out_shape=(jax.ShapeDtype...]
where the time goes in v3:
time: 129 us
  Pallas kernels  127 us (98%)
    pallas_call x1, Pallas kernels, run_front(): pl.pallas_call(functools.partial(front, sizes), out_shape=(jax.ShapeDtype...  107 us
    pallas_call x1, Pallas kernels, run_finish(): pl.pallas_call(finish, out_shape=(jax.ShapeDtypeStruct(e.shape, F32), jax...  20.8 us

profile of v3, /device:TPU:0, one launch (start us, length us, event | category | flops | bytes accessed | tf_op | source)
XLA Modules:
  0.0 128.7 jit_solution(12658658483248383570)
XLA Ops:
  0.6 106.6 %front.1 = (bf16[96,4096]{1,0:T(8,128)(2,1)}, f32[32,2048]{1,0:T(8,128)}, bf16[96,2048]{1,0:T(8,128)(2,1)}, f32[4096,2048]{1,0:T(8,128)S(1)}, bf16[512,4096]{1,0...) custom-call(bf16[128,4096]{1,0:T(8,128)(2,1)} %a_ref.1, bf16[256,2048]{1,0:T(8,128)(2,1)} %g_ref.1, f32[32,2048]{1,0:T(8,128)} %bitcast.7, ...), custom_call_target="tpu_custom_call" | custom-call | flops 99999997952 | bytes 67108864 | tf_op jit(solution)/shard_map/front/pallas_call | solution.py:385
  107.2 0.0 copy-start
  107.2 20.8 %finish.1 = (f32[4096,2048]{1,0:T(8,128)}, bf16[4096,2048]{1,0:T(8,128)(2,1)}) custom-call(bf16[512,4096]{1,0:T(8,128)(2,1)S(1)} %get-tuple-element.11.a_ref, bf16[512,2048]{1,0:T(8,128)(2,1)S(1)} %get-tuple-element.12.g_ref, f32[4096,2048]{1,0:T(8,128)S(1)} %get-tuple-element.13.e_ref, bf16[96,4096]{1,0:T(8,128)(2,1)} %get-tuple-element.14.q_ref, ...), custom_call_target="tpu_custom_call" | custom-call | tf_op jit(solution)/shard_map/finish/pallas_call | solution.py:445
  128.0 0.0 copy-done
  128.0 0.7 copy.8
Async XLA Ops:
  107.2 20.8 %copy-start = (f32[32,2048]{1,0:T(8,128)S(1)}, f32[32,2048]{1,0:T(8,128)}, u32[]{:S(2)}) copy-start(f32[32,2048]{1,0:T(8,128)} %get-tuple-element.18) | copy-start | bytes 786436
